TPU v7x, 32 devices: a whole 2x2x4 slice. The times are simulated.
32 devices in a mesh: groups: 2 (over x), rows: 8 (over z, y), chan: 2 (over core).
Axes of the slice: x: 2, y: 2, z: 4, core: 2. Of those that a mesh axis runs over, the one named last changes fastest.
Arguments:
- latents: bfloat16 [48, 32, 1024], P('groups', 'rows', 'chan'), parts along dimension 0, may hold values from -6 to 6
- timestep: int32 [6], P('groups'), parts along dimension 0, may hold values from 0 to 999
- label: int32 [6], P('groups'), parts along dimension 0, may hold values from 0 to 15
- time_table: bfloat16 [1000, 1024], P(None, 'chan'), may hold values from -3 to 3
- class_table: bfloat16 [16, 1024], replicated, may hold values from -6 to 6
- dw_kernel: bfloat16 [7, 7, 1024], P(None, None, 'chan'), may hold values from -0.875 to 0.875
- dw_bias: bfloat16 [1024], P('chan'), may hold values from -3 to 3
- ln_gain: bfloat16 [1024], P('chan'), may hold values from 0.25 to 1.75
- ln_bias: bfloat16 [1024], P('chan'), may hold values from -2 to 2
- up_weight: bfloat16 [1024, 4096], P(None, 'chan'), may hold values from -0.1875 to 0.1875
- up_bias: bfloat16 [4096], P('chan'), may hold values from -3 to 3
- down_weight: bfloat16 [4096, 1024], P('chan'), may hold values from -0.09375 to 0.09375
- down_bias: bfloat16 [1024], P('chan'), may hold values from -3 to 3
- layer_scale: bfloat16 [1024], replicated, may hold values from 0.5 to 1.5
Outputs:
- features: bfloat16 [48, 32, 1024], P(('groups', 'rows'), None, 'chan'), parts along dimension 0
- gradient: float32 [48, 32, 1024], P('groups', 'rows', 'chan'), parts along dimension 0
There are 2 independent parts, one for each index of `groups`. A program takes and returns all parts, laid end to end along the dimension named above; an argument that names none is the same for every part. Nothing has to cross between parts.
Inputs may be any that keep to these rules, and one draw needn't show every extreme that they name: One timestep index for each image, a row of the table of 1000 timesteps. `label`: one defect class for each image, out of 16 classes.
All inputs are finite; a program needn't handle non-finite values.
Results may differ from a plain program's by a relative error of at most 0.0045.
Values may be sent and summed in bfloat16 or wider, within the bound.
No kernel may reach another device: no remote copies, remote signals or barrier semaphores. Data moves between devices by JAX's collectives and lax.ppermute only.
A program may use at most 128 MiB of HBM per device.

v0:
```python
import jax
import jax.numpy as jnp
from jax import lax
from jax.sharding import PartitionSpec as P

KAPPA = 0.7978845608028654
EPSILON = 1e-06


def with_halo(cells, sides, width):
    for axis, dim in sides:
        count = lax.axis_size(axis)
        ends = count - 1
        head = lax.slice_in_dim(cells, 0, width, axis=dim)
        tail = lax.slice_in_dim(cells, cells.shape[dim] - width, cells.shape[dim], axis=dim)
        cells = jnp.concatenate(
            [
                lax.ppermute(tail, axis, [(i, (i + 1) % count) for i in range(ends)]),
                cells,
                lax.ppermute(head, axis, [((i + 1) % count, i) for i in range(ends)]),
            ],
            axis=dim,
        )
    return cells


def gelu_tanh(values):
    inner = KAPPA * (values + 0.044715 * values * values * values)
    return 0.5 * values * (1.0 + jnp.tanh(inner))


def gelu_slope(values):
    tangent = jnp.tanh(KAPPA * (values + 0.044715 * values * values * values))
    return 0.5 * (1.0 + tangent) + 0.5 * values * (1.0 - tangent * tangent) * KAPPA * (
        1.0 + 3.0 * 0.044715 * values * values
    )


def stencil(padded, kernel, masks):
    height = padded.shape[0] - 6
    width = padded.shape[1] - 6
    total = jnp.zeros((height, width, padded.shape[2]), jnp.float32)
    for row_tap in range(7):
        partial_row = jnp.zeros((height, width, padded.shape[2]), jnp.float32)
        for col_tap in range(7):
            partial_row = (
                partial_row
                + padded[row_tap : row_tap + height, col_tap : col_tap + width, :]
                * kernel[row_tap, col_tap]
            )
        total = total + partial_row * masks[row_tap][:, None, None]
    return total


def exact_dot(left, right):
    return jnp.dot(left, right, precision=lax.Precision.HIGHEST, preferred_element_type=jnp.float32)


def local_block(
    latent_pad,
    row_first,
    col_first,
    total_rows,
    total_cols,
    pad_grad,
    time_rows,
    class_half,
    slope_image,
    scale_half,
    dw_kernel,
    dw_bias,
    ln_gain,
    ln_bias,
    up_weight,
    up_bias,
    down_weight,
    down_bias,
    full_channels,
):
    pad_rows = latent_pad.shape[0]
    pad_cols = latent_pad.shape[1]
    height = pad_rows - 6
    width = pad_cols - 6
    channels = latent_pad.shape[2]
    images = time_rows.shape[0]
    image_height = total_rows // images
    row_global = row_first - 3 + jnp.arange(pad_rows, dtype=jnp.int32)
    row_image = jnp.floor_divide(row_global, image_height)
    col_global = col_first - 3 + jnp.arange(pad_cols, dtype=jnp.int32)
    col_valid = ((col_global >= 0) & (col_global < total_cols)).astype(jnp.float32)
    image_hot = (row_image[:, None] == jnp.arange(images, dtype=jnp.int32)[None, :]).astype(
        jnp.float32
    )
    time_pad = exact_dot(image_hot, time_rows)
    start_pad = latent_pad.astype(jnp.float32) + time_pad[:, None, :] * col_valid[None, :, None]
    masks = jnp.stack(
        [
            (row_image[tap : tap + height] == row_image[3 : 3 + height]).astype(jnp.float32)
            for tap in range(7)
        ]
    )
    kernel = dw_kernel.astype(jnp.float32)
    mixed = stencil(start_pad, kernel, masks) + dw_bias.astype(jnp.float32)
    tokens = height * width
    flat = mixed.reshape(tokens, channels)
    first_sum, second_sum = lax.psum((jnp.sum(flat, 1), jnp.sum(flat * flat, 1)), "chan")
    mean = first_sum / full_channels
    variance = second_sum / full_channels - mean * mean
    inverse = lax.rsqrt(variance + EPSILON)
    normed = (flat - mean[:, None]) * inverse[:, None]
    gain = ln_gain.astype(jnp.float32)
    scaled = (normed * gain + ln_bias.astype(jnp.float32)).astype(jnp.bfloat16)
    hidden = jnp.dot(
        lax.all_gather(scaled, "chan", axis=1, tiled=True),
        up_weight,
        preferred_element_type=jnp.float32,
    )
    hidden = hidden + up_bias.astype(jnp.float32)
    active = gelu_tanh(hidden).astype(jnp.bfloat16)
    branch = lax.psum_scatter(
        jnp.dot(active, down_weight, preferred_element_type=jnp.float32),
        "chan",
        scatter_dimension=1,
        tiled=True,
    )
    branch = branch + down_bias.astype(jnp.float32)
    start_cells = start_pad[3 : 3 + height, 3 : 3 + width].reshape(tokens, channels)
    features = (
        (start_cells + scale_half * branch).astype(jnp.bfloat16).reshape(height, width, channels)
    )
    token_image = image_hot[3 : 3 + height]
    slope_rows = exact_dot(token_image, slope_image)
    slope_tokens = jnp.broadcast_to(
        slope_rows[:, None, :], (height, width, slope_rows.shape[1])
    ).reshape(tokens, slope_rows.shape[1])
    hidden_grad = (slope_tokens * gelu_slope(hidden)).astype(jnp.bfloat16)
    grad_terms = lax.dot_general(
        hidden_grad, up_weight, (((1,), (1,)), ((), ())), preferred_element_type=jnp.float32
    )
    normed_grad = lax.psum_scatter(
        grad_terms.astype(jnp.bfloat16), "chan", scatter_dimension=1, tiled=True
    ).astype(jnp.float32)
    gained = normed_grad * gain
    grad_first, grad_second = lax.psum((jnp.sum(gained, 1), jnp.sum(gained * normed, 1)), "chan")
    mixed_grad = inverse[:, None] * (
        gained - grad_first[:, None] / full_channels - normed * grad_second[:, None] / full_channels
    )
    grad_pad = pad_grad(mixed_grad.reshape(height, width, channels))
    class_tokens = exact_dot(token_image, class_half)
    gradient = stencil(grad_pad, kernel[::-1, ::-1], masks) + class_tokens[:, None, :]
    return (features, gradient)


def per_device(
    latents,
    timestep,
    label,
    time_table,
    class_table,
    dw_kernel,
    dw_bias,
    ln_gain,
    ln_bias,
    up_weight,
    up_bias,
    down_weight,
    down_bias,
    layer_scale,
):
    channels = ln_gain.shape[0]
    full_channels = class_table.shape[1]
    half_index = lax.axis_index("chan")
    scale_full = layer_scale.astype(jnp.float32)
    scale_half = lax.dynamic_slice_in_dim(scale_full, half_index * channels, channels, 0)
    time_hot = (
        timestep[:, None] == jnp.arange(time_table.shape[0], dtype=jnp.int32)[None, :]
    ).astype(jnp.float32)
    time_rows = exact_dot(time_hot, time_table.astype(jnp.float32))
    class_hot = (
        label[:, None] == jnp.arange(class_table.shape[0], dtype=jnp.int32)[None, :]
    ).astype(jnp.float32)
    class_rows = exact_dot(class_hot, class_table.astype(jnp.float32))
    class_half = lax.dynamic_slice_in_dim(class_rows, half_index * channels, channels, 1)
    direction = (class_rows * scale_full).astype(jnp.bfloat16)
    slope_image = lax.dot_general(
        direction, down_weight, (((1,), (1,)), ((), ())), preferred_element_type=jnp.float32
    )
    latent_rows = lax.all_to_all(latents, "rows", split_axis=0, concat_axis=1, tiled=True)
    height = latent_rows.shape[0]
    width = latent_rows.shape[1]
    row_first = lax.axis_index("rows") * height
    col_first = 0
    total_rows = height * lax.axis_size("rows")
    latent_pad = with_halo(latent_rows, (("rows", 0),), 3)
    latent_pad = jnp.pad(latent_pad, ((0, 0), (3, 3), (0, 0)))

    def pad_grad(field):
        padded = with_halo(field.astype(jnp.bfloat16), (("rows", 0),), 3).astype(field.dtype)
        return jnp.pad(padded, ((0, 0), (3, 3), (0, 0)))

    features, gradient = local_block(
        latent_pad,
        row_first,
        col_first,
        total_rows,
        width,
        pad_grad,
        time_rows,
        class_half,
        slope_image,
        scale_half,
        dw_kernel,
        dw_bias,
        ln_gain,
        ln_bias,
        up_weight,
        up_bias,
        down_weight,
        down_bias,
        full_channels,
    )
    gradient = lax.all_to_all(gradient, "rows", split_axis=1, concat_axis=0, tiled=True)
    return (features, gradient)


def solution(mesh):
    in_specs = (
        P("groups", "rows", "chan"),
        P("groups"),
        P("groups"),
        P(None, "chan"),
        P(),
        P(None, None, "chan"),
        P("chan"),
        P("chan"),
        P("chan"),
        P(None, "chan"),
        P("chan"),
        P("chan", None),
        P("chan"),
        P(),
    )
    out_specs = (P(("groups", "rows"), None, "chan"), P("groups", "rows", "chan"))
    return jax.shard_map(
        per_device, mesh=mesh, in_specs=in_specs, out_specs=out_specs, check_vma=False
    )
```

profile of v0, /device:TPU:0, one launch (start us, length us, event | category | flops | bytes accessed | tf_op | source)
XLA Modules:
  0.0 107.5 jit_solution(14234665979605698154)
XLA Ops:
  7.2 7.5 %all-to-all-start = ((bf16[24,4,512]{2,1,0:T(4,128)(2,1)}), bf16[24,4,512]{2,1,0:T(4,128)(2,1)S(1)}, u32[]{:S(2)}, u32[]{:S(2)}) async-start(bf16[24,4,512]{2,1,0:T(4,128)(2,1)} %param.14), calls=%async_computation | async-start | bytes 196608 | tf_op jit(solution)/shard_map/all_to_all | solution.py:188
  15.8 1.1 %fusion.183 = (f32[1,1,512]{2,1,0:T(1,128)S(1)}, f32[1,1,512]{2,1,0:T(1,128)S(1)}, f32[1,1,512]{2,1,0:T(1,128)S(1)}, f32[1,1,512]{2,1,0:T(1,128)S(1)}, f32[1,1,5...) fusion(bf16[7,7,512]{2,1,0:T(8,128)(2,1)} %param.19), kind=kLoop, calls=%fused_computation.314 | loop fusion | bytes 77824 | tf_op jit(solution)/shard_map/slice | solution.py:49
  17.1 1.6 %fusion.182 = (f32[1,1,512]{2,1,0:T(1,128)S(1)}, f32[1,1,512]{2,1,0:T(1,128)S(1)}, f32[1,1,512]{2,1,0:T(1,128)S(1)}, f32[1,1,512]{2,1,0:T(1,128)S(1)}, f32[1,1,5...) fusion(bf16[7,7,512]{2,1,0:T(8,128)(2,1)} %param.19), kind=kLoop, calls=%fused_computation.313 | loop fusion | bytes 77824 | tf_op jit(solution)/shard_map/slice | solution.py:49
  23.7 3.4 %fusion.164 = f32[3,2048]{1,0:T(4,128)S(1)} fusion(bf16[2048,1024]{1,0:T(8,128)(2,1)} %param.25, f32[3,1024]{1,0:T(4,128)S(1)} %fusion.169, f32[1024]{0:T(1024)S(1)} %convert_element_type.93), kind=kOutput, calls=%fused_computation.280 | convolution fusion | flops 12589056 | bytes 4235264 | tf_op jit(solution)/shard_map/dot_general | solution.py:185
  28.0 1.3 %collective-permute-start.1 = (bf16[3,32,512]{2,0,1:T(4,128)(2,1)S(1)}, bf16[3,32,512]{2,0,1:T(4,128)(2,1)S(1)}, u32[]{:S(2)}, u32[]{:S(2)}) collective-permute-start(bf16[3,32,512]{2,0,1:T(4,128)(2,1)S(1)} %bitcast.86), channel_id=1, source_target_pairs={{2,0},{4,2},{6,4},{8,6},{10,8},{12,10},{14,12},{3,1},{5,3},{7,5},{... | collective-permute-start | bytes 294920 | tf_op jit(solution)/shard_map/ppermute | solution.py:20
  29.3 4.6 %collective-permute-start = (bf16[3,32,512]{2,0,1:T(4,128)(2,1)S(1)}, bf16[3,32,512]{2,0,1:T(4,128)(2,1)S(1)}, u32[]{:S(2)}, u32[]{:S(2)}) collective-permute-start(bf16[3,32,512]{2,0,1:T(4,128)(2,1)S(1)} %bitcast.87), channel_id=1, source_target_pairs={{0,2},{2,4},{4,6},{6,8},{8,10},{10,12},{12,14},{1,3},{3,5},{5,7},{... | collective-permute-start | bytes 294920 | tf_op jit(solution)/shard_map/ppermute | solution.py:18
  33.9 1.0 collective-permute-done.1
  34.9 2.9 %collective-permute-done = bf16[3,32,512]{2,0,1:T(4,128)(2,1)S(1)} collective-permute-done((bf16[3,32,512]{2,0,1:T(4,128)(2,1)S(1)}, bf16[3,32,512]{2,0,1:T(4,128)(2,1)S(1)}, u32[]{:S(2)}, u32[]{:S(2)}) %collective-permute-start) | collective-permute-done | bytes 98336 | tf_op jit(solution)/shard_map/ppermute | solution.py:18
  38.6 5.1 %fusion.180 = (f32[3,32]{0,1:T(8,128)S(1)}, f32[3,32]{0,1:T(8,128)S(1)}, f32[3,32,512]{2,0,1:T(4,128)S(1)}) fusion(f32[512]{0:T(512)S(1)} %convert_element_type.101, f32[3]{0:T(128)} %get-tuple-element.67, f32[512]{0:T(512)S(1)} %bitcast.113, f32[9,38,512]{2,0,1:T(8,128)S(1)} %multiply_add_fusion, f32[512]{0:T(512)S(1)} %bitcast.111, f32[512]{0:T(512)S(1)} %bitcast.109, ...), kind=kLoop, calls=%fused_computation.312 | loop fusion | flops 5259072 | bytes 9933640 | tf_op jit(solution)/shard_map/reduce_sum | solution.py:106
  44.0 2.5 %all-reduce.3 = (f32[96]{0:T(128)S(1)}, f32[96]{0:T(128)S(1)}) all-reduce(f32[96]{0:T(128)S(1)} %reduce_sum.43, f32[96]{0:T(128)S(1)} %reduce_sum.41), channel_id=1, replica_groups=mesh['groups'=2,'rows'=8,'chan'=2] {'chan'}, use_global_device_ids=true, to_apply=%region_3.4 | all-reduce | flops 192 | bytes 1536 | tf_op jit(solution)/shard_map/psum | solution.py:106
  46.6 1.9 %all_gather.3 = bf16[96,1024]{1,0:T(8,128)(2,1)S(1)} all-gather(bf16[96,512]{1,0:T(8,128)(2,1)S(1)} %add_convert_fusion), channel_id=1, replica_groups=mesh['groups'=2,'rows'=8,'chan'=2] {'chan'}, dimensions={1}, use_global_device_ids=true | all-gather | bytes 294912 | tf_op jit(solution)/shard_map/all_gather | solution.py:114
  48.6 3.6 %fusion.7 = (bf16[96,2048]{1,0:T(8,128)(2,1)S(1)}, f32[96,2048]{1,0:T(8,128)S(1)}) fusion(f32[3,2048]{1,0:T(4,128)S(1)} %fusion.171, f32[2048]{0:T(1024)S(1)} %convert_element_type.105, bf16[96,1024]{1,0:T(8,128)(2,1)S(1)} %all_gather.3, bf16[1024,2048]{1,0:T(8,128)(2,1)} %param.23), kind=kOutput, calls=%fused_computation.56 | convolution fusion | flops 406585344 | bytes 5603328 | tf_op jit(solution)/shard_map/dot_general | solution.py:113
  52.2 2.1 %convolution_convert_fusion = bf16[96,1024]{1,0:T(8,128)(2,1)} fusion(bf16[96,2048]{1,0:T(8,128)(2,1)S(1)} %get-tuple-element.68, bf16[1024,2048]{1,0:T(8,128)(2,1)S(1)} %copy-done.1), kind=kOutput, calls=%fused_computation.49 | convolution fusion | flops 402751488 | bytes 4784128 | tf_op jit(solution)/shard_map/dot_general | solution.py:137
  54.5 9.4 %reduce-scatter.5.cloned.1.call-done = bf16[96,512]{1,0:T(8,128)(2,1)} async-done(((bf16[96,1024]{1,0:T(8,128)(2,1)}), bf16[96,512]{1,0:T(8,128)(2,1)}) %reduce-scatter.5.cloned.1.call-update) | async-done | bytes 98320 | tf_op jit(solution)/shard_map/reduce_scatter | solution.py:140
  63.9 1.1 %fusion.162 = (f32[96]{0:T(128)S(1)}, f32[96]{0:T(128)S(1)}) fusion(bf16[96,512]{1,0:T(8,128)(2,1)} %reduce-scatter.5.cloned.1.call-done, f32[512]{0:T(512)S(1)} %convert_element_type.102, f32[96]{0:T(128)S(1)} %get-tuple-element.61, f32[96]{0:T(128)S(1)} %get-tuple-element.60, f32[3,32,512]{2,1,0:T(8,128)S(1)} %copy.27), kind=kLoop, calls=%fused_computation.275 | loop fusion | flops 343872 | bytes 298496 | tf_op jit(solution)/shard_map/reduce_sum | solution.py:144
  65.0 2.5 %all-reduce.2 = (f32[96]{0:T(128)S(1)}, f32[96]{0:T(128)S(1)}) all-reduce(f32[96]{0:T(128)S(1)} %get-tuple-element.5, f32[96]{0:T(128)S(1)} %get-tuple-element.4), channel_id=1, replica_groups=mesh['groups'=2,'rows'=8,'chan'=2] {'chan'}, use_global_device_ids=true, to_apply=%region_9.10 | all-reduce | flops 192 | bytes 1536 | tf_op jit(solution)/shard_map/psum | solution.py:144
  67.5 1.0 multiply_convert_fusion.2
  68.6 1.3 %collective-permute-start.3 = (bf16[3,32,512]{2,0,1:T(4,128)(2,1)S(1)}, bf16[3,32,512]{2,0,1:T(4,128)(2,1)S(1)}, u32[]{:S(2)}, u32[]{:S(2)}) collective-permute-start(bf16[3,32,512]{2,0,1:T(4,128)(2,1)S(1)} %copy.30), channel_id=1, source_target_pairs={{2,0},{4,2},{6,4},{8,6},{10,8},{12,10},{14,12},{3,1},{5,3},{7,5},{... | collective-permute-start | bytes 294920 | tf_op jit(solution)/shard_map/ppermute | solution.py:20
  69.9 4.6 %collective-permute-start.2 = (bf16[3,32,512]{2,0,1:T(4,128)(2,1)S(1)}, bf16[3,32,512]{2,0,1:T(4,128)(2,1)S(1)}, u32[]{:S(2)}, u32[]{:S(2)}) collective-permute-start(bf16[3,32,512]{2,0,1:T(4,128)(2,1)S(1)} %copy.30), channel_id=1, source_target_pairs={{0,2},{2,4},{4,6},{6,8},{8,10},{10,12},{12,14},{1,3},{3,5},{5,7},{... | collective-permute-start | bytes 294920 | tf_op jit(solution)/shard_map/ppermute | solution.py:18
  74.5 3.8 %fusion.13 = f32[96,1024]{1,0:T(8,128)} fusion(bf16[2048,1024]{1,0:T(8,128)(2,1)} %param.25, f32[96,2048]{1,0:T(8,128)S(1)} %get-tuple-element.69), kind=kOutput, calls=%fused_computation.64 | convolution fusion | flops 404422656 | bytes 5373952 | tf_op jit(solution)/shard_map/dot_general | solution.py:121
  79.9 5.3 %add_add_fusion = f32[3,32,512]{2,0,1:T(4,128)} fusion(f32[9,32,512]{2,0,1:T(8,128)S(1)} %maximum_convert_fusion, f32[3,512]{1,0:T(4,128)S(1)} %fusion.165, f32[3]{0:T(128)} %get-tuple-element.67, f32[512]{0:T(512)S(1)} %bitcast.114, f32[512]{0:T(512)S(1)} %bitcast.112, f32[512]{0:T(512)S(1)} %bitcast.110, f32[512]{0:T(512)S(1)} %bitcast.108, ...), kind=kLoop, calls=%fused_computation.266 | loop fusion | flops 5111808 | bytes 3188808 | tf_op jit(solution)/shard_map/add | solution.py:150
  85.2 5.9 %all-to-all-start.1 = ((f32[3,32,512]{2,0,1:T(4,128)}), f32[3,32,512]{2,0,1:T(4,128)S(1)}, u32[]{:S(2)}, u32[]{:S(2)}) async-start(f32[3,32,512]{2,0,1:T(4,128)} %add_add_fusion), calls=%async_computation.3 | async-start | bytes 524288 | tf_op jit(solution)/shard_map/all_to_all | solution.py:222
  92.1 1.6 %fusion.161 = bf16[96,512]{1,0:T(8,128)(2,1)} fusion(f32[3,32,512]{2,1,0:T(8,128)S(1)} %copy.26, f32[96,512]{1,0:T(8,128)} %reduce-scatter.3.cloned.1.call-done, f32[512]{0:T(512)S(1)} %convert_element_type.107, f32[512]{0:T(512)S(1)} %dynamic_slice.6), kind=kLoop, calls=%fused_computation.271 | loop fusion | flops 196608 | bytes 495616 | tf_op jit(solution)/shard_map/convert_element_type | solution.py:129
  93.7 6.3 %all-to-all-done.1 = f32[3,32,512]{2,0,1:T(4,128)S(1)} async-done(((f32[3,32,512]{2,0,1:T(4,128)}), f32[3,32,512]{2,0,1:T(4,128)S(1)}, u32[]{:S(2)}, u32[]{:S(2)}) %all-to-all-start.1) | async-done | bytes 196640 | tf_op jit(solution)/shard_map/all_to_all | solution.py:222
  (206 shorter events, 10.7 us)
Async XLA Ops:
  7.2 20.8 %all-to-all-start = ((bf16[24,4,512]{2,1,0:T(4,128)(2,1)}), bf16[24,4,512]{2,1,0:T(4,128)(2,1)S(1)}, u32[]{:S(2)}, u32[]{:S(2)}) async-start(bf16[24,4,512]{2,1,0:T(4,128)(2,1)} %param.14), calls=%async_computation | async-start | bytes 196608 | tf_op jit(solution)/shard_map/all_to_all | solution.py:188
  14.7 49.3 %reduce-scatter.5.cloned.1.call-start = ((), (), s32[]{:S(2)}) async-start(), calls=%async_computation.5 | async-start | bytes 294912 | tf_op jit(solution)/shard_map/reduce_scatter | solution.py:140
  15.7 22.5 %copy-start.2 = (f32[1,1,512]{2,1,0:T(1,128)}, f32[1,1,512]{2,1,0:T(1,128)S(1)}, u32[]{:S(2)}) copy-start(f32[1,1,512]{2,1,0:T(1,128)S(1)} %get-tuple-element.51) | copy-start | bytes 6148
  15.7 22.5 %copy-start.4 = (f32[1,1,512]{2,1,0:T(1,128)}, f32[1,1,512]{2,1,0:T(1,128)S(1)}, u32[]{:S(2)}) copy-start(f32[1,1,512]{2,1,0:T(1,128)S(1)} %get-tuple-element.52) | copy-start | bytes 6148
  15.7 22.5 %copy-start.6 = (f32[1,1,512]{2,1,0:T(1,128)}, f32[1,1,512]{2,1,0:T(1,128)S(1)}, u32[]{:S(2)}) copy-start(f32[1,1,512]{2,1,0:T(1,128)S(1)} %get-tuple-element.53) | copy-start | bytes 6148
  15.7 22.5 %copy-start.8 = (f32[1,1,512]{2,1,0:T(1,128)}, f32[1,1,512]{2,1,0:T(1,128)S(1)}, u32[]{:S(2)}) copy-start(f32[1,1,512]{2,1,0:T(1,128)S(1)} %get-tuple-element.54) | copy-start | bytes 6148
  15.7 22.5 %copy-start.10 = (f32[1,1,512]{2,1,0:T(1,128)}, f32[1,1,512]{2,1,0:T(1,128)S(1)}, u32[]{:S(2)}) copy-start(f32[1,1,512]{2,1,0:T(1,128)S(1)} %get-tuple-element.55) | copy-start | bytes 6148
  15.7 22.5 %copy-start.12 = (f32[1,1,512]{2,1,0:T(1,128)}, f32[1,1,512]{2,1,0:T(1,128)S(1)}, u32[]{:S(2)}) copy-start(f32[1,1,512]{2,1,0:T(1,128)S(1)} %get-tuple-element.56) | copy-start | bytes 6148
  15.7 22.5 %copy-start.14 = (f32[1,1,512]{2,1,0:T(1,128)}, f32[1,1,512]{2,1,0:T(1,128)S(1)}, u32[]{:S(2)}) copy-start(f32[1,1,512]{2,1,0:T(1,128)S(1)} %get-tuple-element.57) | copy-start | bytes 6148
  15.8 22.5 %copy-start.16 = (f32[1,1,512]{2,1,0:T(1,128)}, f32[1,1,512]{2,1,0:T(1,128)S(1)}, u32[]{:S(2)}) copy-start(f32[1,1,512]{2,1,0:T(1,128)S(1)} %get-tuple-element.58) | copy-start | bytes 6148
  15.8 22.5 %copy-start.18 = (f32[1,1,512]{2,1,0:T(1,128)}, f32[1,1,512]{2,1,0:T(1,128)S(1)}, u32[]{:S(2)}) copy-start(f32[1,1,512]{2,1,0:T(1,128)S(1)} %get-tuple-element.59) | copy-start | bytes 6148
  16.9 21.3 %copy-start.20 = (f32[1,1,512]{2,1,0:T(1,128)}, f32[1,1,512]{2,1,0:T(1,128)S(1)}, u32[]{:S(2)}) copy-start(f32[1,1,512]{2,1,0:T(1,128)S(1)} %get-tuple-element.30) | copy-start | bytes 6148
  16.9 21.3 %copy-start.22 = (f32[1,1,512]{2,1,0:T(1,128)}, f32[1,1,512]{2,1,0:T(1,128)S(1)}, u32[]{:S(2)}) copy-start(f32[1,1,512]{2,1,0:T(1,128)S(1)} %get-tuple-element.31) | copy-start | bytes 6148
  16.9 21.3 %copy-start.24 = (f32[1,1,512]{2,1,0:T(1,128)}, f32[1,1,512]{2,1,0:T(1,128)S(1)}, u32[]{:S(2)}) copy-start(f32[1,1,512]{2,1,0:T(1,128)S(1)} %get-tuple-element.32) | copy-start | bytes 6148
  16.9 21.3 %copy-start.26 = (f32[1,1,512]{2,1,0:T(1,128)}, f32[1,1,512]{2,1,0:T(1,128)S(1)}, u32[]{:S(2)}) copy-start(f32[1,1,512]{2,1,0:T(1,128)S(1)} %get-tuple-element.33) | copy-start | bytes 6148
  17.0 21.3 %copy-start.28 = (f32[1,1,512]{2,1,0:T(1,128)}, f32[1,1,512]{2,1,0:T(1,128)S(1)}, u32[]{:S(2)}) copy-start(f32[1,1,512]{2,1,0:T(1,128)S(1)} %get-tuple-element.34) | copy-start | bytes 6148
  17.0 21.3 %copy-start.30 = (f32[1,1,512]{2,1,0:T(1,128)}, f32[1,1,512]{2,1,0:T(1,128)S(1)}, u32[]{:S(2)}) copy-start(f32[1,1,512]{2,1,0:T(1,128)S(1)} %get-tuple-element.35) | copy-start | bytes 6148
  17.0 21.3 %copy-start.32 = (f32[1,1,512]{2,1,0:T(1,128)}, f32[1,1,512]{2,1,0:T(1,128)S(1)}, u32[]{:S(2)}) copy-start(f32[1,1,512]{2,1,0:T(1,128)S(1)} %get-tuple-element.36) | copy-start | bytes 6148
  28.0 6.9 %collective-permute-start.1 = (bf16[3,32,512]{2,0,1:T(4,128)(2,1)S(1)}, bf16[3,32,512]{2,0,1:T(4,128)(2,1)S(1)}, u32[]{:S(2)}, u32[]{:S(2)}) collective-permute-start(bf16[3,32,512]{2,0,1:T(4,128)(2,1)S(1)} %bitcast.86), channel_id=1, source_target_pairs={{2,0},{4,2},{6,4},{8,6},{10,8},{12,10},{14,12},{3,1},{5,3},{7,5},{... | collective-permute-start | bytes 294920 | tf_op jit(solution)/shard_map/ppermute | solution.py:20
  29.3 8.5 %collective-permute-start = (bf16[3,32,512]{2,0,1:T(4,128)(2,1)S(1)}, bf16[3,32,512]{2,0,1:T(4,128)(2,1)S(1)}, u32[]{:S(2)}, u32[]{:S(2)}) collective-permute-start(bf16[3,32,512]{2,0,1:T(4,128)(2,1)S(1)} %bitcast.87), channel_id=1, source_target_pairs={{0,2},{2,4},{4,6},{6,8},{8,10},{10,12},{12,14},{1,3},{3,5},{5,7},{... | collective-permute-start | bytes 294920 | tf_op jit(solution)/shard_map/ppermute | solution.py:18
  54.3 37.8 %reduce-scatter.3.cloned.1.call-start = ((), (), s32[]{:S(2)}) async-start(), calls=%async_computation.4 | async-start | bytes 589824 | tf_op jit(solution)/shard_map/reduce_scatter | solution.py:120
  68.6 10.1 %collective-permute-start.3 = (bf16[3,32,512]{2,0,1:T(4,128)(2,1)S(1)}, bf16[3,32,512]{2,0,1:T(4,128)(2,1)S(1)}, u32[]{:S(2)}, u32[]{:S(2)}) collective-permute-start(bf16[3,32,512]{2,0,1:T(4,128)(2,1)S(1)} %copy.30), channel_id=1, source_target_pairs={{2,0},{4,2},{6,4},{8,6},{10,8},{12,10},{14,12},{3,1},{5,3},{7,5},{... | collective-permute-start | bytes 294920 | tf_op jit(solution)/shard_map/ppermute | solution.py:20
  69.9 9.3 %collective-permute-start.2 = (bf16[3,32,512]{2,0,1:T(4,128)(2,1)S(1)}, bf16[3,32,512]{2,0,1:T(4,128)(2,1)S(1)}, u32[]{:S(2)}, u32[]{:S(2)}) collective-permute-start(bf16[3,32,512]{2,0,1:T(4,128)(2,1)S(1)} %copy.30), channel_id=1, source_target_pairs={{0,2},{2,4},{4,6},{6,8},{8,10},{10,12},{12,14},{1,3},{3,5},{5,7},{... | collective-permute-start | bytes 294920 | tf_op jit(solution)/shard_map/ppermute | solution.py:18
  85.2 14.7 %all-to-all-start.1 = ((f32[3,32,512]{2,0,1:T(4,128)}), f32[3,32,512]{2,0,1:T(4,128)S(1)}, u32[]{:S(2)}, u32[]{:S(2)}) async-start(f32[3,32,512]{2,0,1:T(4,128)} %add_add_fusion), calls=%async_computation.3 | async-start | bytes 524288 | tf_op jit(solution)/shard_map/all_to_all | solution.py:222
  (67 other events, 582.4 us)
Sparse Core Ops, SparseCore 0:
  54.4 9.4 reduce-scatter.4
  78.8 8.9 reduce-scatter.2
where the time goes:
time: 109 us; the launch traced here: 108 us
  starting transfers between devices  25.1 us (23%)
  waiting for transfers between devices  20.2 us (19%)
  other arithmetic  19.8 us (18%)
  between operations  15.5 us (14%)
  matrix products  14.5 us (13%)
  blocking collectives  6.89 us (6%)
  local copies, waits for them, and re-layouts  5.62 us (5%)
    reduce_scatter x1, waiting for transfers between devices, local_block(): lax.psum_scatter(grad_terms.astype(jnp.bfloat16), 'chan', scatter_dimensi...  9.45 us
    ppermute x2, starting transfers between devices, with_halo(): lax.ppermute(tail, axis, [(i, (i + 1) % count) for i in range(ends)])  9.11 us
    all_to_all x1, starting transfers between devices, per_device(): lax.all_to_all(latents, 'rows', split_axis=0, concat_axis=1, tiled=True)  7.45 us
    all_to_all x1, waiting for transfers between devices, per_device(): lax.all_to_all(gradient, 'rows', split_axis=1, concat_axis=0, tiled=True)  6.28 us
    all_to_all x1, starting transfers between devices, per_device(): lax.all_to_all(gradient, 'rows', split_axis=1, concat_axis=0, tiled=True)  5.88 us
    add x1, other arithmetic, local_block(): stencil(grad_pad, kernel[::-1, ::-1], masks) + class_tokens[:, None, :]  5.34 us
    reduce_sum x1, other arithmetic, local_block(): jnp.sum(flat, 1)  5.05 us
    dot_general x1, matrix products, local_block(): jnp.dot(active, down_weight, preferred_element_type=jnp.float32)  3.82 us
  transfers between devices with their start and end apart: 8, of which 5 were waited for; matrix products, arithmetic and copies ran while one was open for 23% of the time, Pallas kernels for 0%

commit v1 on v0

--- a/solution.py
+++ b/solution.py
@@ -185,7 +185,19 @@
     slope_image = lax.dot_general(
         direction, down_weight, (((1,), (1,)), ((), ())), preferred_element_type=jnp.float32
     )
-    latent_rows = lax.all_to_all(latents, "rows", split_axis=0, concat_axis=1, tiled=True)
+    ways, here = (lax.axis_size("rows"), lax.axis_index("rows"))
+    width_2 = latents.shape[0] // ways
+    shape = list(latents.shape)
+    shape[0] = width_2
+    height_2 = shape[1]
+    shape[1] = height_2 * ways
+    full = jnp.zeros(shape, latents.dtype)
+    for mask in range(ways):
+        part = lax.dynamic_slice_in_dim(latents, (here ^ mask) * width_2, width_2, axis=0)
+        if mask:
+            part = lax.ppermute(part, "rows", [(d, d ^ mask) for d in range(ways)])
+        full = lax.dynamic_update_slice_in_dim(full, part, (here ^ mask) * height_2, axis=1)
+    latent_rows = full
     height = latent_rows.shape[0]
     width = latent_rows.shape[1]
     row_first = lax.axis_index("rows") * height

time: 109 us -> 117 us (1.073)
  starting transfers between devices: 25.1 us -> 30.7 us
  other arithmetic: 19.8 us -> 17.5 us
  waiting for transfers between devices: 20.2 us -> 22.5 us
  matrix products: 14.5 us -> 15.9 us
    ppermute x0 -> x7, starting transfers between devices: none -> 12.9 us  [per_device(): part = lax.ppermute(part, 'rows', [(d, d ^ mask) for d in range(ways)])]
    all_to_all x1 -> x0, starting transfers between devices: 7.45 us -> none  [per_device(): lax.all_to_all(latents, 'rows', split_axis=0, concat_axis=1, tiled=True)]
    ppermute x0 -> x7, waiting for transfers between devices: none -> 6.3 us  [per_device(): part = lax.ppermute(part, 'rows', [(d, d ^ mask) for d in range(ways)])]
    reduce_scatter x1, waiting for transfers between devices: 9.45 us -> 7.03 us  [local_block(): lax.psum_scatter(grad_terms.astype(jnp.bfloat16), 'chan', scatter_dimensi...]
    ppermute x2, waiting for transfers between devices: 3.39 us -> 1.82 us  [with_halo(): lax.ppermute(tail, axis, [(i, (i + 1) % count) for i in range(ends)])]
    dot_general x5, matrix products: 1.62 us -> 2.98 us  [exact_dot(): jnp.dot(left, right, precision=lax.Precision.HIGHEST, preferred_element_t...]
  transfers between devices with their start and end apart: 8 -> 14, of which waited for: 5 -> 7; matrix products, arithmetic and copies ran while one was open for 23% -> 21% of each run, Pallas kernels for 0% -> 0%
where the time goes in v1:
time: 117 us; the launch traced here: 116 us
  starting transfers between devices  30.7 us (26%)
  waiting for transfers between devices  22.5 us (19%)
  other arithmetic  17.5 us (15%)
  matrix products  15.9 us (14%)
  between operations  15.7 us (13%)
  blocking collectives  6.89 us (6%)
  local copies, waits for them, and re-layouts  6.71 us (6%)
    ppermute x7, starting transfers between devices, per_device(): part = lax.ppermute(part, 'rows', [(d, d ^ mask) for d in range(ways)])  12.9 us
    ppermute x2, starting transfers between devices, with_halo(): lax.ppermute(tail, axis, [(i, (i + 1) % count) for i in range(ends)])  9.29 us
    reduce_scatter x1, waiting for transfers between devices, local_block(): lax.psum_scatter(grad_terms.astype(jnp.bfloat16), 'chan', scatter_dimensi...  7.03 us
    ppermute x7, waiting for transfers between devices, per_device(): part = lax.ppermute(part, 'rows', [(d, d ^ mask) for d in range(ways)])  6.3 us
    all_to_all x1, waiting for transfers between devices, per_device(): lax.all_to_all(gradient, 'rows', split_axis=1, concat_axis=0, tiled=True)  6.28 us
    all_to_all x1, starting transfers between devices, per_device(): lax.all_to_all(gradient, 'rows', split_axis=1, concat_axis=0, tiled=True)  5.89 us
    add x1, other arithmetic, local_block(): stencil(grad_pad, kernel[::-1, ::-1], masks) + class_tokens[:, None, :]  5.27 us
    reduce_sum x1, other arithmetic, local_block(): jnp.sum(flat, 1)  5.01 us
  transfers between devices with their start and end apart: 14, of which 7 were waited for; matrix products, arithmetic and copies ran while one was open for 21% of the time, Pallas kernels for 0%

profile of v1, /device:TPU:0, one launch (start us, length us, event | category | flops | bytes accessed | tf_op | source)
XLA Modules:
  0.0 115.9 jit_solution(4038298779071343087)
XLA Ops:
  8.2 3.1 %collective-permute-start = (bf16[3,4,512]{2,0,1:T(4,128)(2,1)S(1)}, bf16[3,4,512]{2,0,1:T(4,128)(2,1)S(1)}, u32[]{:S(2)}, u32[]{:S(2)}) collective-permute-start(bf16[3,4,512]{2,0,1:T(4,128)(2,1)S(1)} %copy.48), channel_id=1, source_target_pairs={{0,2},{2,0},{4,6},{6,4},{8,10},{10,8},{12,14},{14,12},{1,3},{3,1},... | collective-permute-start | bytes 36872 | tf_op jit(solution)/shard_map/ppermute | solution.py:198
  11.3 1.6 %collective-permute-start.1 = (bf16[3,4,512]{2,0,1:T(4,128)(2,1)S(1)}, bf16[3,4,512]{2,0,1:T(4,128)(2,1)S(1)}, u32[]{:S(2)}, u32[]{:S(2)}) collective-permute-start(bf16[3,4,512]{2,0,1:T(4,128)(2,1)S(1)} %copy.49), channel_id=1, source_target_pairs={{0,4},{2,6},{4,0},{6,2},{8,12},{10,14},{12,8},{14,10},{1,5},{3,7},... | collective-permute-start | bytes 36872 | tf_op jit(solution)/shard_map/ppermute | solution.py:198
  13.0 3.0 %collective-permute-start.3 = (bf16[3,4,512]{2,0,1:T(4,128)(2,1)S(1)}, bf16[3,4,512]{2,0,1:T(4,128)(2,1)S(1)}, u32[]{:S(2)}, u32[]{:S(2)}) collective-permute-start(bf16[3,4,512]{2,0,1:T(4,128)(2,1)S(1)} %copy.51), channel_id=1, source_target_pairs={{0,8},{2,10},{4,12},{6,14},{8,0},{10,2},{12,4},{14,6},{1,9},{3,11}... | collective-permute-start | bytes 36872 | tf_op jit(solution)/shard_map/ppermute | solution.py:198
  16.1 1.4 %collective-permute-start.4 = (bf16[3,4,512]{2,0,1:T(4,128)(2,1)S(1)}, bf16[3,4,512]{2,0,1:T(4,128)(2,1)S(1)}, u32[]{:S(2)}, u32[]{:S(2)}) collective-permute-start(bf16[3,4,512]{2,0,1:T(4,128)(2,1)S(1)} %copy.52), channel_id=1, source_target_pairs={{0,10},{2,8},{4,14},{6,12},{8,2},{10,0},{12,6},{14,4},{1,11},{3,9}... | collective-permute-start | bytes 36872 | tf_op jit(solution)/shard_map/ppermute | solution.py:198
  19.8 1.6 %fusion.182 = (f32[1,1,512]{2,1,0:T(1,128)S(1)}, f32[1,1,512]{2,1,0:T(1,128)S(1)}, f32[1,1,512]{2,1,0:T(1,128)S(1)}, f32[1,1,512]{2,1,0:T(1,128)S(1)}, f32[1,1,5...) fusion(bf16[7,7,512]{2,1,0:T(8,128)(2,1)} %param.19), kind=kLoop, calls=%fused_computation.329 | loop fusion | bytes 77824 | tf_op jit(solution)/shard_map/slice | solution.py:49
  24.3 3.4 %fusion.164 = f32[3,2048]{1,0:T(4,128)S(1)} fusion(bf16[2048,1024]{1,0:T(8,128)(2,1)} %param.25, f32[3,1024]{1,0:T(4,128)S(1)} %fusion.170, f32[1024]{0:T(1024)S(1)} %convert_element_type.93), kind=kOutput, calls=%fused_computation.281 | convolution fusion | flops 12589056 | bytes 4235264 | tf_op jit(solution)/shard_map/dot_general | solution.py:185
  29.4 3.7 %collective-permute-start.5 = (bf16[3,4,512]{2,0,1:T(4,128)(2,1)S(1)}, bf16[3,4,512]{2,0,1:T(4,128)(2,1)S(1)}, u32[]{:S(2)}, u32[]{:S(2)}) collective-permute-start(bf16[3,4,512]{2,0,1:T(4,128)(2,1)S(1)} %copy.53), channel_id=1, source_target_pairs={{0,12},{2,14},{4,8},{6,10},{8,4},{10,6},{12,0},{14,2},{1,13},{3,15... | collective-permute-start | bytes 36872 | tf_op jit(solution)/shard_map/ppermute | solution.py:198
  33.3 1.7 %collective-permute-done.5 = bf16[3,4,512]{2,0,1:T(4,128)(2,1)S(1)} collective-permute-done((bf16[3,4,512]{2,0,1:T(4,128)(2,1)S(1)}, bf16[3,4,512]{2,0,1:T(4,128)(2,1)S(1)}, u32[]{:S(2)}, u32[]{:S(2)}) %collective-permute-start.5) | collective-permute-done | bytes 12320 | tf_op jit(solution)/shard_map/ppermute | solution.py:198
  35.1 4.6 %collective-permute-done.6 = bf16[3,4,512]{2,0,1:T(4,128)(2,1)S(1)} collective-permute-done((bf16[3,4,512]{2,0,1:T(4,128)(2,1)S(1)}, bf16[3,4,512]{2,0,1:T(4,128)(2,1)S(1)}, u32[]{:S(2)}, u32[]{:S(2)}) %collective-permute-start.6) | collective-permute-done | bytes 12320 | tf_op jit(solution)/shard_map/ppermute | solution.py:198
  40.9 4.6 %collective-permute-start.7 = (bf16[3,32,512]{2,0,1:T(4,128)(2,1)S(1)}, bf16[3,32,512]{2,0,1:T(4,128)(2,1)S(1)}, u32[]{:S(2)}, u32[]{:S(2)}) collective-permute-start(bf16[3,32,512]{2,0,1:T(4,128)(2,1)S(1)} %constant_dynamic-update-slice_fusion), channel_id=1, source_target_pairs={{0,2},{2,4},{4,6},{6,8},{8,10},{10,12},{12,14},{1,3},{3,5},{5,7},{... | collective-permute-start | bytes 294920 | tf_op jit(solution)/shard_map/ppermute | solution.py:18
  46.5 1.5 %collective-permute-done.7 = bf16[3,32,512]{2,0,1:T(4,128)(2,1)S(1)} collective-permute-done((bf16[3,32,512]{2,0,1:T(4,128)(2,1)S(1)}, bf16[3,32,512]{2,0,1:T(4,128)(2,1)S(1)}, u32[]{:S(2)}, u32[]{:S(2)}) %collective-permute-start.7) | collective-permute-done | bytes 98336 | tf_op jit(solution)/shard_map/ppermute | solution.py:18
  48.8 5.0 %fusion.180 = (f32[3,32]{0,1:T(8,128)S(1)}, f32[3,32]{0,1:T(8,128)S(1)}, f32[3,32,512]{2,0,1:T(4,128)S(1)}) fusion(f32[512]{0:T(512)S(1)} %convert_element_type.101, f32[3]{0:T(128)} %get-tuple-element.75, f32[512]{0:T(512)S(1)} %bitcast.105, f32[9,38,512]{2,0,1:T(8,128)S(1)} %multiply_add_fusion, f32[512]{0:T(512)S(1)} %bitcast.103, f32[512]{0:T(512)S(1)} %bitcast.101, ...), kind=kLoop, calls=%fused_computation.328 | loop fusion | flops 5259072 | bytes 9933640 | tf_op jit(solution)/shard_map/reduce_sum | solution.py:106
  54.2 2.5 %all-reduce.3 = (f32[96]{0:T(128)S(1)}, f32[96]{0:T(128)S(1)}) all-reduce(f32[96]{0:T(128)S(1)} %reduce_sum.43, f32[96]{0:T(128)S(1)} %reduce_sum.41), channel_id=1, replica_groups=mesh['groups'=2,'rows'=8,'chan'=2] {'chan'}, use_global_device_ids=true, to_apply=%region_3.4 | all-reduce | flops 192 | bytes 1536 | tf_op jit(solution)/shard_map/psum | solution.py:106
  56.8 1.9 %all_gather.3 = bf16[96,1024]{1,0:T(8,128)(2,1)S(1)} all-gather(bf16[96,512]{1,0:T(8,128)(2,1)S(1)} %add_convert_fusion), channel_id=1, replica_groups=mesh['groups'=2,'rows'=8,'chan'=2] {'chan'}, dimensions={1}, use_global_device_ids=true | all-gather | bytes 294912 | tf_op jit(solution)/shard_map/all_gather | solution.py:114
  58.7 3.6 %fusion.7 = (bf16[96,2048]{1,0:T(8,128)(2,1)S(1)}, f32[96,2048]{1,0:T(8,128)S(1)}) fusion(f32[3,2048]{1,0:T(4,128)S(1)} %fusion.172, f32[2048]{0:T(1024)S(1)} %convert_element_type.105, bf16[96,1024]{1,0:T(8,128)(2,1)S(1)} %all_gather.3, bf16[1024,2048]{1,0:T(8,128)(2,1)} %param.23), kind=kOutput, calls=%fused_computation.56 | convolution fusion | flops 406585344 | bytes 5603328 | tf_op jit(solution)/shard_map/dot_general | solution.py:113
  62.3 2.1 %convolution_convert_fusion = bf16[96,1024]{1,0:T(8,128)(2,1)} fusion(bf16[96,2048]{1,0:T(8,128)(2,1)S(1)} %get-tuple-element.76, bf16[1024,2048]{1,0:T(8,128)(2,1)S(1)} %copy-done.1), kind=kOutput, calls=%fused_computation.49 | convolution fusion | flops 402751488 | bytes 4784128 | tf_op jit(solution)/shard_map/dot_general | solution.py:137
  65.3 7.0 %reduce-scatter.5.cloned.1.call-done = bf16[96,512]{1,0:T(8,128)(2,1)} async-done(((bf16[96,1024]{1,0:T(8,128)(2,1)}), bf16[96,512]{1,0:T(8,128)(2,1)}) %reduce-scatter.5.cloned.1.call-update) | async-done | bytes 98320 | tf_op jit(solution)/shard_map/reduce_scatter | solution.py:140
  73.5 2.5 %all-reduce.2 = (f32[96]{0:T(128)S(1)}, f32[96]{0:T(128)S(1)}) all-reduce(f32[96]{0:T(128)S(1)} %get-tuple-element.5, f32[96]{0:T(128)S(1)} %get-tuple-element.4), channel_id=1, replica_groups=mesh['groups'=2,'rows'=8,'chan'=2] {'chan'}, use_global_device_ids=true, to_apply=%region_9.10 | all-reduce | flops 192 | bytes 1536 | tf_op jit(solution)/shard_map/psum | solution.py:144
  78.4 4.7 %collective-permute-start.9 = (bf16[3,32,512]{2,0,1:T(4,128)(2,1)S(1)}, bf16[3,32,512]{2,0,1:T(4,128)(2,1)S(1)}, u32[]{:S(2)}, u32[]{:S(2)}) collective-permute-start(bf16[3,32,512]{2,0,1:T(4,128)(2,1)S(1)} %copy.43), channel_id=1, source_target_pairs={{0,2},{2,4},{4,6},{6,8},{8,10},{10,12},{12,14},{1,3},{3,5},{5,7},{... | collective-permute-start | bytes 294920 | tf_op jit(solution)/shard_map/ppermute | solution.py:18
  83.1 3.8 %fusion.13 = f32[96,1024]{1,0:T(8,128)} fusion(bf16[2048,1024]{1,0:T(8,128)(2,1)} %param.25, f32[96,2048]{1,0:T(8,128)S(1)} %get-tuple-element.77), kind=kOutput, calls=%fused_computation.64 | convolution fusion | flops 404422656 | bytes 5373952 | tf_op jit(solution)/shard_map/dot_general | solution.py:121
  88.3 5.3 %add_add_fusion = f32[3,32,512]{2,0,1:T(4,128)} fusion(f32[9,32,512]{2,0,1:T(8,128)S(1)} %maximum_convert_fusion, f32[3,512]{1,0:T(4,128)S(1)} %fusion.165, f32[3]{0:T(128)} %get-tuple-element.75, f32[512]{0:T(512)S(1)} %bitcast.106, f32[512]{0:T(512)S(1)} %bitcast.104, f32[512]{0:T(512)S(1)} %bitcast.102, f32[512]{0:T(512)S(1)} %bitcast.100, ...), kind=kLoop, calls=%fused_computation.266 | loop fusion | flops 5111808 | bytes 3188808 | tf_op jit(solution)/shard_map/add | solution.py:150
  93.6 5.9 %all-to-all-start = ((f32[3,32,512]{2,0,1:T(4,128)}), f32[3,32,512]{2,0,1:T(4,128)S(1)}, u32[]{:S(2)}, u32[]{:S(2)}) async-start(f32[3,32,512]{2,0,1:T(4,128)} %add_add_fusion), calls=%async_computation.2 | async-start | bytes 524288 | tf_op jit(solution)/shard_map/all_to_all | solution.py:234
  100.4 1.6 %fusion.161 = bf16[96,512]{1,0:T(8,128)(2,1)} fusion(f32[3,32,512]{2,1,0:T(8,128)S(1)} %copy.39, f32[96,512]{1,0:T(8,128)} %reduce-scatter.3.cloned.1.call-done, f32[512]{0:T(512)S(1)} %convert_element_type.107, f32[512]{0:T(512)S(1)} %dynamic_slice.38), kind=kLoop, calls=%fused_computation.271 | loop fusion | flops 196608 | bytes 495616 | tf_op jit(solution)/shard_map/convert_element_type | solution.py:129
  102.0 6.3 %all-to-all-done = f32[3,32,512]{2,0,1:T(4,128)S(1)} async-done(((f32[3,32,512]{2,0,1:T(4,128)}), f32[3,32,512]{2,0,1:T(4,128)S(1)}, u32[]{:S(2)}, u32[]{:S(2)}) %all-to-all-start) | async-done | bytes 196640 | tf_op jit(solution)/shard_map/all_to_all | solution.py:234
  (242 shorter events, 17.9 us)
Async XLA Ops:
  7.2 65.2 %reduce-scatter.5.cloned.1.call-start = ((), (), s32[]{:S(2)}) async-start(), calls=%async_computation.4 | async-start | bytes 294912 | tf_op jit(solution)/shard_map/reduce_scatter | solution.py:140
  8.2 21.2 %collective-permute-start = (bf16[3,4,512]{2,0,1:T(4,128)(2,1)S(1)}, bf16[3,4,512]{2,0,1:T(4,128)(2,1)S(1)}, u32[]{:S(2)}, u32[]{:S(2)}) collective-permute-start(bf16[3,4,512]{2,0,1:T(4,128)(2,1)S(1)} %copy.48), channel_id=1, source_target_pairs={{0,2},{2,0},{4,6},{6,4},{8,10},{10,8},{12,14},{14,12},{1,3},{3,1},... | collective-permute-start | bytes 36872 | tf_op jit(solution)/shard_map/ppermute | solution.py:198
  11.3 21.8 %collective-permute-start.1 = (bf16[3,4,512]{2,0,1:T(4,128)(2,1)S(1)}, bf16[3,4,512]{2,0,1:T(4,128)(2,1)S(1)}, u32[]{:S(2)}, u32[]{:S(2)}) collective-permute-start(bf16[3,4,512]{2,0,1:T(4,128)(2,1)S(1)} %copy.49), channel_id=1, source_target_pairs={{0,4},{2,6},{4,0},{6,2},{8,12},{10,14},{12,8},{14,10},{1,5},{3,7},... | collective-permute-start | bytes 36872 | tf_op jit(solution)/shard_map/ppermute | solution.py:198
  12.9 20.3 %collective-permute-start.2 = (bf16[3,4,512]{2,0,1:T(4,128)(2,1)S(1)}, bf16[3,4,512]{2,0,1:T(4,128)(2,1)S(1)}, u32[]{:S(2)}, u32[]{:S(2)}) collective-permute-start(bf16[3,4,512]{2,0,1:T(4,128)(2,1)S(1)} %copy.50), channel_id=1, source_target_pairs={{0,6},{2,4},{4,2},{6,0},{8,14},{10,12},{12,10},{14,8},{1,7},{3,5},... | collective-permute-start | bytes 36872 | tf_op jit(solution)/shard_map/ppermute | solution.py:198
  13.0 20.2 %collective-permute-start.3 = (bf16[3,4,512]{2,0,1:T(4,128)(2,1)S(1)}, bf16[3,4,512]{2,0,1:T(4,128)(2,1)S(1)}, u32[]{:S(2)}, u32[]{:S(2)}) collective-permute-start(bf16[3,4,512]{2,0,1:T(4,128)(2,1)S(1)} %copy.51), channel_id=1, source_target_pairs={{0,8},{2,10},{4,12},{6,14},{8,0},{10,2},{12,4},{14,6},{1,9},{3,11}... | collective-permute-start | bytes 36872 | tf_op jit(solution)/shard_map/ppermute | solution.py:198
  16.1 17.2 %collective-permute-start.4 = (bf16[3,4,512]{2,0,1:T(4,128)(2,1)S(1)}, bf16[3,4,512]{2,0,1:T(4,128)(2,1)S(1)}, u32[]{:S(2)}, u32[]{:S(2)}) collective-permute-start(bf16[3,4,512]{2,0,1:T(4,128)(2,1)S(1)} %copy.52), channel_id=1, source_target_pairs={{0,10},{2,8},{4,14},{6,12},{8,2},{10,0},{12,6},{14,4},{1,11},{3,9}... | collective-permute-start | bytes 36872 | tf_op jit(solution)/shard_map/ppermute | solution.py:198
  18.4 30.0 %copy-start.2 = (f32[1,1,512]{2,1,0:T(1,128)}, f32[1,1,512]{2,1,0:T(1,128)S(1)}, u32[]{:S(2)}) copy-start(f32[1,1,512]{2,1,0:T(1,128)S(1)} %get-tuple-element.65) | copy-start | bytes 6148
  18.4 30.0 %copy-start.4 = (f32[1,1,512]{2,1,0:T(1,128)}, f32[1,1,512]{2,1,0:T(1,128)S(1)}, u32[]{:S(2)}) copy-start(f32[1,1,512]{2,1,0:T(1,128)S(1)} %get-tuple-element.66) | copy-start | bytes 6148
  18.4 30.0 %copy-start.6 = (f32[1,1,512]{2,1,0:T(1,128)}, f32[1,1,512]{2,1,0:T(1,128)S(1)}, u32[]{:S(2)}) copy-start(f32[1,1,512]{2,1,0:T(1,128)S(1)} %get-tuple-element.67) | copy-start | bytes 6148
  19.6 28.8 %copy-start.8 = (f32[1,1,512]{2,1,0:T(1,128)}, f32[1,1,512]{2,1,0:T(1,128)S(1)}, u32[]{:S(2)}) copy-start(f32[1,1,512]{2,1,0:T(1,128)S(1)} %get-tuple-element.38) | copy-start | bytes 6148
  19.6 28.8 %copy-start.10 = (f32[1,1,512]{2,1,0:T(1,128)}, f32[1,1,512]{2,1,0:T(1,128)S(1)}, u32[]{:S(2)}) copy-start(f32[1,1,512]{2,1,0:T(1,128)S(1)} %get-tuple-element.39) | copy-start | bytes 6148
  19.6 28.8 %copy-start.12 = (f32[1,1,512]{2,1,0:T(1,128)}, f32[1,1,512]{2,1,0:T(1,128)S(1)}, u32[]{:S(2)}) copy-start(f32[1,1,512]{2,1,0:T(1,128)S(1)} %get-tuple-element.40) | copy-start | bytes 6148
  19.6 28.8 %copy-start.14 = (f32[1,1,512]{2,1,0:T(1,128)}, f32[1,1,512]{2,1,0:T(1,128)S(1)}, u32[]{:S(2)}) copy-start(f32[1,1,512]{2,1,0:T(1,128)S(1)} %get-tuple-element.41) | copy-start | bytes 6148
  19.6 28.8 %copy-start.16 = (f32[1,1,512]{2,1,0:T(1,128)}, f32[1,1,512]{2,1,0:T(1,128)S(1)}, u32[]{:S(2)}) copy-start(f32[1,1,512]{2,1,0:T(1,128)S(1)} %get-tuple-element.42) | copy-start | bytes 6148
  19.6 28.8 %copy-start.18 = (f32[1,1,512]{2,1,0:T(1,128)}, f32[1,1,512]{2,1,0:T(1,128)S(1)}, u32[]{:S(2)}) copy-start(f32[1,1,512]{2,1,0:T(1,128)S(1)} %get-tuple-element.43) | copy-start | bytes 6148
  19.6 28.8 %copy-start.20 = (f32[1,1,512]{2,1,0:T(1,128)}, f32[1,1,512]{2,1,0:T(1,128)S(1)}, u32[]{:S(2)}) copy-start(f32[1,1,512]{2,1,0:T(1,128)S(1)} %get-tuple-element.44) | copy-start | bytes 6148
  29.4 5.6 %collective-permute-start.5 = (bf16[3,4,512]{2,0,1:T(4,128)(2,1)S(1)}, bf16[3,4,512]{2,0,1:T(4,128)(2,1)S(1)}, u32[]{:S(2)}, u32[]{:S(2)}) collective-permute-start(bf16[3,4,512]{2,0,1:T(4,128)(2,1)S(1)} %copy.53), channel_id=1, source_target_pairs={{0,12},{2,14},{4,8},{6,10},{8,4},{10,6},{12,0},{14,2},{1,13},{3,15... | collective-permute-start | bytes 36872 | tf_op jit(solution)/shard_map/ppermute | solution.py:198
  33.1 6.5 %collective-permute-start.6 = (bf16[3,4,512]{2,0,1:T(4,128)(2,1)S(1)}, bf16[3,4,512]{2,0,1:T(4,128)(2,1)S(1)}, u32[]{:S(2)}, u32[]{:S(2)}) collective-permute-start(bf16[3,4,512]{2,0,1:T(4,128)(2,1)S(1)} %copy.54), channel_id=1, source_target_pairs={{0,14},{2,12},{4,10},{6,8},{8,6},{10,4},{12,2},{14,0},{1,15},{3,13... | collective-permute-start | bytes 36872 | tf_op jit(solution)/shard_map/ppermute | solution.py:198
  39.6 6.9 %collective-permute-start.8 = (bf16[3,32,512]{2,0,1:T(4,128)(2,1)S(1)}, bf16[3,32,512]{2,0,1:T(4,128)(2,1)S(1)}, u32[]{:S(2)}, u32[]{:S(2)}) collective-permute-start(bf16[3,32,512]{2,0,1:T(4,128)(2,1)S(1)} %constant_dynamic-update-slice_fusion), channel_id=1, source_target_pairs={{2,0},{4,2},{6,4},{8,6},{10,8},{12,10},{14,12},{3,1},{5,3},{7,5},{... | collective-permute-start | bytes 294920 | tf_op jit(solution)/shard_map/ppermute | solution.py:20
  40.9 7.1 %collective-permute-start.7 = (bf16[3,32,512]{2,0,1:T(4,128)(2,1)S(1)}, bf16[3,32,512]{2,0,1:T(4,128)(2,1)S(1)}, u32[]{:S(2)}, u32[]{:S(2)}) collective-permute-start(bf16[3,32,512]{2,0,1:T(4,128)(2,1)S(1)} %constant_dynamic-update-slice_fusion), channel_id=1, source_target_pairs={{0,2},{2,4},{4,6},{6,8},{8,10},{10,12},{12,14},{1,3},{3,5},{5,7},{... | collective-permute-start | bytes 294920 | tf_op jit(solution)/shard_map/ppermute | solution.py:18
  64.5 36.0 %reduce-scatter.3.cloned.1.call-start = ((), (), s32[]{:S(2)}) async-start(), calls=%async_computation.3 | async-start | bytes 589824 | tf_op jit(solution)/shard_map/reduce_scatter | solution.py:120
  77.1 10.2 %collective-permute-start.10 = (bf16[3,32,512]{2,0,1:T(4,128)(2,1)S(1)}, bf16[3,32,512]{2,0,1:T(4,128)(2,1)S(1)}, u32[]{:S(2)}, u32[]{:S(2)}) collective-permute-start(bf16[3,32,512]{2,0,1:T(4,128)(2,1)S(1)} %copy.43), channel_id=1, source_target_pairs={{2,0},{4,2},{6,4},{8,6},{10,8},{12,10},{14,12},{3,1},{5,3},{7,5},{... | collective-permute-start | bytes 294920 | tf_op jit(solution)/shard_map/ppermute | solution.py:20
  78.4 9.3 %collective-permute-start.9 = (bf16[3,32,512]{2,0,1:T(4,128)(2,1)S(1)}, bf16[3,32,512]{2,0,1:T(4,128)(2,1)S(1)}, u32[]{:S(2)}, u32[]{:S(2)}) collective-permute-start(bf16[3,32,512]{2,0,1:T(4,128)(2,1)S(1)} %copy.43), channel_id=1, source_target_pairs={{0,2},{2,4},{4,6},{6,8},{8,10},{10,12},{12,14},{1,3},{3,5},{5,7},{... | collective-permute-start | bytes 294920 | tf_op jit(solution)/shard_map/ppermute | solution.py:18
  93.6 14.7 %all-to-all-start = ((f32[3,32,512]{2,0,1:T(4,128)}), f32[3,32,512]{2,0,1:T(4,128)S(1)}, u32[]{:S(2)}, u32[]{:S(2)}) async-start(f32[3,32,512]{2,0,1:T(4,128)} %add_add_fusion), calls=%async_computation.2 | async-start | bytes 524288 | tf_op jit(solution)/shard_map/all_to_all | solution.py:234
  (77 other events, 933.9 us)
Sparse Core Ops, SparseCore 0:
  64.6 7.7 reduce-scatter.4
  87.4 8.8 reduce-scatter.2
